TPU v7x, 256 devices: a whole 4x4x8 slice. The times are simulated.
256 devices in a mesh: grp: 8 (over z), ep: 32 (over y, x, core).
Axes of the slice: x: 4, y: 4, z: 8, core: 2. Of those that a mesh axis runs over, the one named last changes fastest.
Arguments:
- pol_hidden: bfloat16 [10240, 1024], P(('grp', 'ep')), may hold values from -80 to 80
- ref_hidden: bfloat16 [10240, 1024], P(('grp', 'ep')), may hold values from -80 to 80
- pol_routes: int32 [10240, 8], P(('grp', 'ep')), may hold values from 0 to 63, all different within a row; in each aligned block of 40 rows (0 to 39, 40 to 79, ...) at most 7 rows name the same one
- ref_routes: int32 [10240, 8], P(('grp', 'ep')), may hold values from 0 to 63, all different within a row; in each aligned block of 40 rows (0 to 39, 40 to 79, ...) at most 7 rows name the same one
- pol_gates: float32 [10240, 8], P(('grp', 'ep')), may hold values from 0.02 to 0.3
- ref_gates: float32 [10240, 8], P(('grp', 'ep')), may hold values from 0.02 to 0.3
- w_gate: bfloat16 [64, 1024, 384], P('ep'), may hold values from -0.1875 to 0.1875
- w_up: bfloat16 [64, 1024, 384], P('ep'), may hold values from -0.1875 to 0.1875
- w_down: bfloat16 [64, 384, 1024], P('ep'), may hold values from -0.3125 to 0.3125
- norm_gain: float32 [1024], replicated, may hold values from 0.5 to 1.5
- vocab_head: bfloat16 [77824, 1024], P(('grp', 'ep')), may hold values from -2 to 2
- targets: int32 [10240], P(('grp', 'ep')), may hold values from 0 to 77823
- seq_lengths: int32 [256], replicated, may hold values from 1 to 1024, 10240 in all
- owners: int32 [256], replicated, may hold values from 0 to 255, each once
Outputs:
- token_ratio: float32 [10240], P(('grp', 'ep'))
- owned_mean: float32 [256], P(('grp', 'ep'))
Inputs may be any that keep to these rules, and one draw needn't show every extreme that they name: `pol_routes`: each row names 8 different experts; among the 40 rows of one device no expert is named by more than 7 rows, a bound that some block reaches. `ref_routes`: each row names 8 different experts; among the 40 rows of one device no expert is named by more than 7 rows, a bound that some block reaches. `seq_lengths`: the lengths sum to 10240; the longest is exactly 1024. `owners`: every device index appears exactly once.
All inputs are finite; a program needn't handle non-finite values.
Results may differ from a plain program's by a relative error of at most 0.0062.
Values may be sent and summed in bfloat16 or wider, within the bound.
A program may use at most 128 MiB of HBM per device.

v0:
```python
import jax
import jax.numpy as jnp
from jax import lax
from jax.sharding import PartitionSpec as P


def joined_2(value, axis, join):
    pieces = jax.tree.map(lambda part: lax.all_gather(part, axis), value)
    head = jax.tree.map(lambda part: part[0], pieces)
    tail = jax.tree.map(lambda part: part[1:], pieces)
    so_far, _ = lax.scan(lambda so_far, share: (join(so_far, share), None), head, tail)
    return so_far


def combine_stats(earlier_part, second):
    peak = jnp.maximum(earlier_part[0], second[0])
    totals = earlier_part[1] * jnp.exp(earlier_part[0] - peak) + second[1] * jnp.exp(
        second[0] - peak
    )
    return (peak, totals, earlier_part[2] + second[2])


def vocab_stats(row_block, weights, vocab_ids, wanted):
    logits = jnp.einsum("td,vd->tv", row_block, weights, preferred_element_type=jnp.float32)
    peak = jnp.max(logits, axis=1)
    totals = jnp.sum(jnp.exp(logits - peak[:, None]), axis=1)
    picked = jnp.sum(jnp.where(vocab_ids[None, :] == wanted[:, None], logits, 0.0), axis=1)
    return (peak, totals, picked)


def expert_tables(routes, gates, experts, capacity):
    route_hits = routes[:, :, None] == jnp.arange(experts, dtype=jnp.int32)[None, None, :]
    members = jnp.sum(route_hits.astype(jnp.int32), axis=1)
    earlier = jnp.cumsum(members, axis=0) - members
    placed = (members[:, :, None] > 0) & (
        earlier[:, :, None] == jnp.arange(capacity, dtype=jnp.int32)[None, None, :]
    )
    weight = jnp.sum(jnp.where(route_hits, gates[:, :, None], 0.0), axis=1)
    tok_count = routes.shape[0]
    picker = placed.astype(jnp.bfloat16).reshape(tok_count, experts * capacity)
    mixing = (weight[:, :, None] * placed.astype(jnp.float32)).reshape(
        tok_count, experts * capacity
    )
    return (picker, mixing)


def local(
    pol_hidden,
    ref_hidden,
    pol_routes,
    ref_routes,
    pol_gates,
    ref_gates,
    w_gate,
    w_up,
    w_down,
    norm_gain,
    vocab_head,
    targets,
    seq_lengths,
    owners,
):
    groups = lax.axis_size("ep")
    device_index = lax.axis_index(("grp", "ep"))
    local_experts = w_gate.shape[0]
    experts = local_experts * groups
    tok_count = pol_hidden.shape[0]
    width = pol_hidden.shape[1]
    fanout = pol_routes.shape[1]
    capacity = tok_count * fanout // experts + 2
    pol_pick, pol_mixing = expert_tables(pol_routes, pol_gates, experts, capacity)
    ref_pick, ref_mixing = expert_tables(ref_routes, ref_gates, experts, capacity)
    pol_send = jnp.einsum(
        "ts,td->sd", pol_pick, pol_hidden, preferred_element_type=jnp.float32
    ).astype(jnp.bfloat16)
    ref_send = jnp.einsum(
        "ts,td->sd", ref_pick, ref_hidden, preferred_element_type=jnp.float32
    ).astype(jnp.bfloat16)
    pol_send = pol_send.reshape(groups, local_experts, capacity, width)
    ref_send = ref_send.reshape(groups, local_experts, capacity, width)
    pol_part = lax.all_to_all(pol_send, "ep", split_axis=0, concat_axis=0, tiled=True)
    ref_part = lax.all_to_all(ref_send, "ep", split_axis=0, concat_axis=0, tiled=True)
    slots = pol_part.shape[2]
    joined = jnp.concatenate((pol_part, ref_part), axis=2)
    gate_act = jnp.einsum("nesd,edf->nesf", joined, w_gate, preferred_element_type=jnp.float32)
    up_act = jnp.einsum("nesd,edf->nesf", joined, w_up, preferred_element_type=jnp.float32)
    inner = (jax.nn.silu(gate_act) * up_act).astype(jnp.bfloat16)
    outputs = jnp.einsum(
        "nesf,efd->nesd", inner, w_down, preferred_element_type=jnp.float32
    ).astype(jnp.bfloat16)
    pol_back = lax.all_to_all(outputs[:, :, :slots], "ep", split_axis=0, concat_axis=0, tiled=True)
    ref_back = lax.all_to_all(outputs[:, :, slots:], "ep", split_axis=0, concat_axis=0, tiled=True)

    def mix_back(hidden, mixing, back):
        rows_back = back.reshape(experts * capacity, width).astype(jnp.float32)
        mixed = hidden.astype(jnp.float32) + jnp.dot(
            mixing, rows_back, precision=lax.Precision.HIGHEST
        )
        scale = lax.rsqrt(jnp.mean(mixed * mixed, axis=1, keepdims=True) + 1e-06)
        return (mixed * scale * norm_gain).astype(jnp.bfloat16)

    pol_normed = mix_back(pol_hidden, pol_mixing, pol_back)
    ref_normed = mix_back(ref_hidden, ref_mixing, ref_back)
    vocab_rows = vocab_head.shape[0]
    band = lax.axis_index("grp")
    pol_col, ref_col, wanted = (
        lax.all_gather(pol_normed, "grp", axis=0, tiled=True),
        lax.all_gather(ref_normed, "grp", axis=0, tiled=True),
        lax.all_gather(targets, "grp", axis=0, tiled=True),
    )
    col_count = wanted.shape[0]
    floor_value = jnp.full((2, col_count), -1e30, jnp.float32)
    blank = jnp.zeros((2, col_count), jnp.float32)
    piece = lax.all_gather(vocab_head, "ep", axis=0, tiled=True)
    count = piece.shape[0]
    place = jnp.arange(count, dtype=jnp.int32)
    vocab_ids = band * groups * vocab_rows + place
    pol_stats = vocab_stats(pol_col, piece, vocab_ids, wanted)
    ref_stats = vocab_stats(ref_col, piece, vocab_ids, wanted)
    fresh = tuple(
        (jnp.stack((pol_part, ref_part)) for pol_part, ref_part in zip(pol_stats, ref_stats))
    )
    stats = combine_stats((floor_value, blank, blank), fresh)
    peak, totals, picked = joined_2(stats, "grp", combine_stats)
    logprob = picked - (peak + jnp.log(totals))
    mine = lax.dynamic_slice_in_dim(logprob, band * tok_count, tok_count, axis=1)
    token_ratio = mine[0] - mine[1]
    offsets = jnp.cumsum(seq_lengths) - seq_lengths
    positions = device_index * tok_count + jnp.arange(tok_count, dtype=jnp.int32)
    inside = (positions[:, None] >= offsets[None, :]) & (
        positions[:, None] < (offsets + seq_lengths)[None, :]
    )
    partial_value = jnp.dot(
        token_ratio, inside.astype(jnp.float32), precision=lax.Precision.HIGHEST
    ) / seq_lengths.astype(jnp.float32)
    sums = lax.psum(partial_value, ("grp", "ep"))
    owned = jnp.sum(jnp.where(owners == device_index, sums, 0.0)).reshape(1)
    return (token_ratio, owned)


def solution(mesh):
    return jax.shard_map(
        local,
        mesh=mesh,
        in_specs=(
            P(("grp", "ep"), None),
            P(("grp", "ep"), None),
            P(("grp", "ep"), None),
            P(("grp", "ep"), None),
            P(("grp", "ep"), None),
            P(("grp", "ep"), None),
            P("ep", None, None),
            P("ep", None, None),
            P("ep", None, None),
            P(),
            P(("grp", "ep"), None),
            P(("grp", "ep")),
            P(),
            P(),
        ),
        out_specs=(P(("grp", "ep")), P(("grp", "ep"))),
        check_vma=False,
    )
```

profile of v0, /device:TPU:1, one launch (start us, length us, event | category | flops | bytes accessed | tf_op | source)
XLA Modules:
  0.0 389.7 jit_solution(15554492775969641314)
XLA Ops:
  11.8 2.0 copy.67
  13.7 8.7 %all-to-all-start = ((bf16[32,2,7,1024]{3,1,2,0:T(2,128)(2,1)}), bf16[32,2,7,1024]{3,1,2,0:T(2,128)(2,1)S(1)}, u32[]{:S(2)}, u32[]{:S(2)}) async-start(bf16[32,2,7,1024]{3,1,2,0:T(2,128)(2,1)} %copy.67), calls=%async_computation | async-start | bytes 1835008 | tf_op jit(solution)/shard_map/all_to_all | solution.py:81
  27.0 2.0 copy.71
  28.9 12.9 %all-to-all-done = bf16[32,2,7,1024]{3,1,2,0:T(2,128)(2,1)S(1)} async-done(((bf16[32,2,7,1024]{3,1,2,0:T(2,128)(2,1)}), bf16[32,2,7,1024]{3,1,2,0:T(2,128)(2,1)S(1)}, u32[]{:S(2)}, u32[]{:S(2)}) %all-to-all-start) | async-done | bytes 917536 | tf_op jit(solution)/shard_map/all_to_all | solution.py:81
  42.7 5.4 %all-to-all-start.1 = ((bf16[32,2,7,1024]{3,1,2,0:T(2,128)(2,1)}), bf16[32,2,7,1024]{3,1,2,0:T(2,128)(2,1)}, u32[]{:S(2)}, u32[]{:S(2)}) async-start(bf16[32,2,7,1024]{3,1,2,0:T(2,128)(2,1)} %copy.71), calls=%async_computation.1 | async-start | bytes 1835008 | tf_op jit(solution)/shard_map/all_to_all | solution.py:82
  49.6 14.5 %all-to-all-done.1 = bf16[32,2,7,1024]{3,1,2,0:T(2,128)(2,1)} async-done(((bf16[32,2,7,1024]{3,1,2,0:T(2,128)(2,1)}), bf16[32,2,7,1024]{3,1,2,0:T(2,128)(2,1)}, u32[]{:S(2)}, u32[]{:S(2)}) %all-to-all-start.1) | async-done | bytes 917536 | tf_op jit(solution)/shard_map/all_to_all | solution.py:82
  65.8 2.2 fusion.9
  68.0 5.2 %convert_bitcast_fusion = bf16[32,2,14,1024]{3,0,2,1:T(8,128)(2,1)} fusion(bf16[2,384,1024]{2,1,0:T(8,128)(2,1)S(1)} %copy-done, bf16[32,2,14,1024]{3,0,2,1:T(8,128)(2,1)S(1)} %copy_dynamic-update-slice_fusion, bf16[2,1024,384]{2,1,0:T(8,128)(2,1)} %param.23, f32[32,2,14,384]{3,0,2,1:T(8,128)} %fusion.9), kind=kOutput, calls=%fused_computation.12 | convolution fusion | flops 1412268032 | bytes 8192000 | tf_op jit(solution)/shard_map/nesf,efd->nesd/dot_general | solution.py:88
  73.2 1.9 fusion.44
  75.2 1.9 copy.78
  77.1 3.9 all-to-all-start.3
  81.8 1.9 copy.74
  83.7 21.1 %all-to-all-done.3 = bf16[32,2,7,1024]{3,1,2,0:T(2,128)(2,1)S(1)} async-done(((bf16[32,2,7,1024]{3,1,2,0:T(2,128)(2,1)}), bf16[32,2,7,1024]{3,1,2,0:T(2,128)(2,1)S(1)}, u32[]{:S(2)}, u32[]{:S(2)}) %all-to-all-start.3) | async-done | bytes 917536 | tf_op jit(solution)/shard_map/all_to_all | solution.py:92
  104.8 6.1 %all-to-all-start.2 = ((bf16[32,2,7,1024]{3,1,2,0:T(2,128)(2,1)}), bf16[32,2,7,1024]{3,1,2,0:T(2,128)(2,1)S(1)}, u32[]{:S(2)}, u32[]{:S(2)}) async-start(bf16[32,2,7,1024]{3,1,2,0:T(2,128)(2,1)} %copy.74), calls=%async_computation.2 | async-start | bytes 1835008 | tf_op jit(solution)/shard_map/all_to_all | solution.py:91
  113.7 20.4 %all-reduce = s32[320]{0:T(512)S(1)} all-reduce(s32[320]{0:T(512)S(1)} %dynamic-update-slice), channel_id=1, replica_groups=mesh['grp'=8,'ep'=32] {'grp'}, use_global_device_ids=true, to_apply=%add | all-reduce | flops 320 | bytes 2560
  141.2 20.2 %all_gather.26 = bf16[320,1024]{1,0:T(8,128)(2,1)S(1)} all-gather(bf16[40,1024]{1,0:T(8,128)(2,1)S(1)} %get-tuple-element.71), channel_id=1, replica_groups=mesh['grp'=8,'ep'=32] {'grp'}, dimensions={0}, use_global_device_ids=true | all-gather | bytes 737280 | tf_op jit(solution)/shard_map/all_gather | solution.py:107
  161.4 20.5 %all_gather.28 = bf16[320,1024]{1,0:T(8,128)(2,1)S(1)} all-gather(bf16[40,1024]{1,0:T(8,128)(2,1)S(1)} %get-tuple-element.72), channel_id=1, replica_groups=mesh['grp'=8,'ep'=32] {'grp'}, dimensions={0}, use_global_device_ids=true | all-gather | bytes 737280 | tf_op jit(solution)/shard_map/all_gather | solution.py:108
  181.9 13.4 %fusion.45 = (f32[320]{0:T(512)S(1)}, f32[320,9728]{1,0:T(8,128)}) fusion(bf16[320,1024]{1,0:T(8,128)(2,1)S(1)} %all_gather.26, bf16[9728,1024]{1,0:T(8,128)(2,1)} %all-gather.4.cloned.1.call-done), kind=kOutput, calls=%fused_computation.84 | convolution fusion | flops 6378454528 | bytes 33031424 | tf_op jit(solution)/shard_map/td,vd->tv/dot_general | solution.py:24
  195.3 13.5 %fusion.46 = (f32[320]{0:T(512)S(1)}, f32[320,9728]{1,0:T(8,128)}) fusion(bf16[320,1024]{1,0:T(8,128)(2,1)S(1)} %all_gather.28, bf16[9728,1024]{1,0:T(8,128)(2,1)} %all-gather.4.cloned.1.call-done), kind=kOutput, calls=%fused_computation.85 | convolution fusion | flops 6378454528 | bytes 33031424 | tf_op jit(solution)/shard_map/td,vd->tv/dot_general | solution.py:24
  208.8 11.5 %fusion.2 = (f32[320]{0:T(512)S(1)}, f32[320]{0:T(512)S(1)}, f32[320]{0:T(512)S(1)}, f32[320]{0:T(512)S(1)}) fusion(f32[320,9728]{1,0:T(8,128)} %get-tuple-element.80, s32[9728]{0:T(1024)S(1)} %copy-done.17, s32[320]{0:T(512)S(1)} %all-reduce, f32[320]{0:T(512)S(1)} %get-tuple-element.79, f32[320,9728]{1,0:T(8,128)} %get-tuple-element.82, ...), kind=kLoop, calls=%fused_computation.8 | loop fusion | flops 28015360 | bytes 24951552 | tf_op jit(solution)/shard_map/reduce_sum | solution.py:27
  220.3 18.0 %all-gather.1 = f32[8,2,320]{2,1,0:T(2,128)S(1)} all-gather(f32[1,2,320]{2,1,0:T(2,128)S(1)} %maximum_bitcast_fusion), channel_id=2, replica_groups=mesh['grp'=8,'ep'=32] {'grp'}, dimensions={0}, use_global_device_ids=true | all-gather | bytes 23040 | tf_op jit(solution)/shard_map/all_gather | solution.py:8
  238.4 18.0 %all_gather.30 = f32[8,2,320]{2,1,0:T(2,128)S(1)} all-gather(f32[1,2,320]{2,1,0:T(2,128)S(1)} %get-tuple-element.73), channel_id=1, replica_groups=mesh['grp'=8,'ep'=32] {'grp'}, dimensions={0}, use_global_device_ids=true | all-gather | bytes 23040 | tf_op jit(solution)/shard_map/all_gather | solution.py:8
  256.5 18.0 %all_gather.29 = f32[8,2,320]{2,1,0:T(2,128)S(1)} all-gather(f32[1,2,320]{2,1,0:T(2,128)S(1)} %get-tuple-element.74), channel_id=1, replica_groups=mesh['grp'=8,'ep'=32] {'grp'}, dimensions={0}, use_global_device_ids=true | all-gather | bytes 23040 | tf_op jit(solution)/shard_map/all_gather | solution.py:8
  275.7 106.6 %psum.7 = f32[256]{0:T(256)S(1)} all-reduce(f32[256]{0:T(256)S(1)} %convert_divide_fusion), channel_id=1, replica_groups=mesh['grp'=8,'ep'=32] {'grp','ep'}, use_global_device_ids=true, to_apply=%region_18.19 | all-reduce | flops 256 | bytes 2048 | tf_op jit(solution)/shard_map/psum | solution.py:136
  (149 shorter events, 24.9 us)
Async XLA Ops:
  7.2 60.8 %copy-start = (bf16[2,384,1024]{2,1,0:T(8,128)(2,1)S(1)}, bf16[2,384,1024]{2,1,0:T(8,128)(2,1)}, u32[]{:S(2)}) copy-start(bf16[2,384,1024]{2,1,0:T(8,128)(2,1)} %param.24) | copy-start | bytes 4718596
  7.2 3.8 copy-start.7
  7.2 174.7 %all-gather.4.cloned.1.call-start = ((), (), s32[]{:S(2)}) async-start(), calls=%async_computation.4 | async-start | bytes 20545536 | tf_op jit(solution)/shard_map/all_gather | solution.py:114
  11.7 10.7 %copy-start.22 = (s32[40,8]{0,1:T(8,128)S(1)}, s32[40,8]{0,1:T(8,128)}, u32[]{:S(2)}) copy-start(s32[40,8]{0,1:T(8,128)} %param.19) | copy-start | bytes 3844
  13.7 10.4 %copy-start.5 = (bf16[40,1024]{1,0:T(8,128)(2,1)S(1)}, bf16[40,1024]{1,0:T(8,128)(2,1)}, u32[]{:S(2)}) copy-start(bf16[40,1024]{1,0:T(8,128)(2,1)} %param.17) | copy-start | bytes 245764
  13.7 10.4 %copy-start.19 = (s32[448]{0:T(512)S(1)}, s32[448]{0:T(512)}, u32[]{:S(2)}) copy-start(s32[448]{0:T(512)} %copy-done.18) | copy-start | bytes 5380
  13.7 28.1 %all-to-all-start = ((bf16[32,2,7,1024]{3,1,2,0:T(2,128)(2,1)}), bf16[32,2,7,1024]{3,1,2,0:T(2,128)(2,1)S(1)}, u32[]{:S(2)}, u32[]{:S(2)}) async-start(bf16[32,2,7,1024]{3,1,2,0:T(2,128)(2,1)} %copy.67), calls=%async_computation | async-start | bytes 1835008 | tf_op jit(solution)/shard_map/all_to_all | solution.py:81
  42.7 21.4 %all-to-all-start.1 = ((bf16[32,2,7,1024]{3,1,2,0:T(2,128)(2,1)}), bf16[32,2,7,1024]{3,1,2,0:T(2,128)(2,1)}, u32[]{:S(2)}, u32[]{:S(2)}) async-start(bf16[32,2,7,1024]{3,1,2,0:T(2,128)(2,1)} %copy.71), calls=%async_computation.1 | async-start | bytes 1835008 | tf_op jit(solution)/shard_map/all_to_all | solution.py:82
  75.2 5.8 %copy-start.23 = (f32[40,8]{0,1:T(8,128)S(1)}, f32[40,8]{0,1:T(8,128)}, u32[]{:S(2)}) copy-start(f32[40,8]{0,1:T(8,128)} %param.21) | copy-start | bytes 3844
  75.2 5.9 %copy-start.16 = (s32[40,8]{1,0:T(8,128)S(1)}, s32[40,8]{1,0:T(8,128)}, u32[]{:S(2)}) copy-start(s32[40,8]{1,0:T(8,128)} %copy-done.15) | copy-start | bytes 3844
  75.2 6.1 %copy-start.12 = (s32[40,64]{0,1:T(8,128)S(1)}, s32[40,64]{0,1:T(8,128)}, u32[]{:S(2)}) copy-start(s32[40,64]{0,1:T(8,128)} %copy-done.11) | copy-start | bytes 30724
  77.1 4.4 %copy-start.24 = (f32[40,8]{0,1:T(8,128)S(1)}, f32[40,8]{0,1:T(8,128)}, u32[]{:S(2)}) copy-start(f32[40,8]{0,1:T(8,128)} %param.20) | copy-start | bytes 3844
  77.1 4.4 %copy-start.14 = (s32[40,8]{1,0:T(8,128)S(1)}, s32[40,8]{1,0:T(8,128)}, u32[]{:S(2)}) copy-start(s32[40,8]{1,0:T(8,128)} %copy-done.13) | copy-start | bytes 3844
  77.1 27.7 %all-to-all-start.3 = ((bf16[32,2,7,1024]{3,1,2,0:T(2,128)(2,1)}), bf16[32,2,7,1024]{3,1,2,0:T(2,128)(2,1)S(1)}, u32[]{:S(2)}, u32[]{:S(2)}) async-start(bf16[32,2,7,1024]{3,1,2,0:T(2,128)(2,1)} %copy.78), calls=%async_computation.3 | async-start | bytes 1835008 | tf_op jit(solution)/shard_map/all_to_all | solution.py:92
  81.8 29.2 %copy-start.10 = (s32[40,64]{0,1:T(8,128)S(1)}, s32[40,64]{0,1:T(8,128)}, u32[]{:S(2)}) copy-start(s32[40,64]{0,1:T(8,128)} %copy-done.9) | copy-start | bytes 30724
  81.8 30.0 %copy-start.20 = (s32[256]{0:T(256)S(1)}, s32[256]{0:T(256)}, u32[]{:S(2)}) copy-start(s32[256]{0:T(256)} %param.28) | copy-start | bytes 3076
  81.8 30.4 %copy-start.28 = (u32[256]{0:T(256)S(1)}, u32[256]{0:T(256)}, u32[]{:S(2)}) copy-start(u32[256]{0:T(256)} %constant.68) | copy-start | bytes 3076
  81.8 31.6 %copy-start.27 = (s32[40]{0:T(128)S(1)}, s32[40]{0:T(128)}, u32[]{:S(2)}) copy-start(s32[40]{0:T(128)} %param.27) | copy-start | bytes 484
  104.8 32.7 %all-to-all-start.2 = ((bf16[32,2,7,1024]{3,1,2,0:T(2,128)(2,1)}), bf16[32,2,7,1024]{3,1,2,0:T(2,128)(2,1)S(1)}, u32[]{:S(2)}, u32[]{:S(2)}) async-start(bf16[32,2,7,1024]{3,1,2,0:T(2,128)(2,1)} %copy.74), calls=%async_computation.2 | async-start | bytes 1835008 | tf_op jit(solution)/shard_map/all_to_all | solution.py:91
  195.3 13.5 %copy-start.17 = (s32[9728]{0:T(1024)S(1)}, s32[9728]{0:T(1024)}, u32[]{:S(2)}) copy-start(s32[9728]{0:T(1024)} %iota_add_fusion) | copy-start | bytes 116740
  208.8 66.7 %copy-start.26 = (s32[256]{0:T(256)S(1)}, s32[256]{0:T(256)}, u32[]{:S(2)}) copy-start(s32[256]{0:T(256)} %get-tuple-element.67) | copy-start | bytes 3076
  208.8 66.7 %copy-start.29 = (s32[40]{0:T(128)S(1)}, s32[40]{0:T(128)}, u32[]{:S(2)}) copy-start(s32[40]{0:T(128)} %iota_add_fusion.1) | copy-start | bytes 484
  208.8 173.4 %copy-start.25 = (s32[256]{0:T(256)S(1)}, s32[256]{0:T(256)}, u32[]{:S(2)}) copy-start(s32[256]{0:T(256)} %param.29) | copy-start | bytes 3076
  208.8 174.0 %copy-start.1 = (bf16[2,384,1024]{2,1,0:T(8,128)(2,1)S(1)}, bf16[2,384,1024]{2,1,0:T(8,128)(2,1)}, u32[]{:S(2)}) copy-start(bf16[2,384,1024]{2,1,0:T(8,128)(2,1)} %param.24) | copy-start | bytes 4718596
  (11 other events, 12.0 us)
Sparse Core Ops, SparseCore 0:
  10.6 105.0 all-gather.3
where the time goes:
time: 391 us; the launch traced here: 390 us
  blocking collectives  222 us (57%)
  waiting for transfers between devices  49.2 us (13%)
  matrix products  38.7 us (10%)
  local copies, waits for them, and re-layouts  24.4 us (6%)
  starting transfers between devices  24.2 us (6%)
  other arithmetic  16.1 us (4%)
  between operations  15.3 us (4%)
    psum x1, blocking collectives, local(): sums = lax.psum(partial_value, ('grp', 'ep'))  107 us
    all_gather x3, blocking collectives, joined_2(): pieces = jax.tree.map(lambda part: lax.all_gather(part, axis), value)  54 us
    dot_general x2, matrix products, vocab_stats(): jnp.einsum('td,vd->tv', row_block, weights, preferred_element_type=jnp.fl...  26.9 us
    all_to_all x1, waiting for transfers between devices, local(): lax.all_to_all(outputs[:, :, slots:], 'ep', split_axis=0, concat_axis=0,...  21.1 us
    all_gather x1, blocking collectives, local(): lax.all_gather(ref_normed, 'grp', axis=0, tiled=True)  20.5 us
    unnamed x1, blocking collectives  20.4 us
    all_gather x1, blocking collectives, local(): lax.all_gather(pol_normed, 'grp', axis=0, tiled=True)  20.2 us
    all_to_all x1, waiting for transfers between devices, local(): lax.all_to_all(ref_send, 'ep', split_axis=0, concat_axis=0, tiled=True)  14.5 us
  transfers between devices with their start and end apart: 5, of which 3 were waited for; matrix products, arithmetic and copies ran while one was open for 9% of the time, Pallas kernels for 0%

commit v1 on v0

--- a/solution.py
+++ b/solution.py
@@ -133,7 +133,9 @@
     partial_value = jnp.dot(
         token_ratio, inside.astype(jnp.float32), precision=lax.Precision.HIGHEST
     ) / seq_lengths.astype(jnp.float32)
-    sums = lax.psum(partial_value, ("grp", "ep"))
+    sums = partial_value
+    for mesh_axis in ("ep", "grp"):
+        sums = lax.psum(sums, mesh_axis)
     owned = jnp.sum(jnp.where(owners == device_index, sums, 0.0)).reshape(1)
     return (token_ratio, owned)
 

time: 391 us -> 392 us (level)
    psum x1 -> x2, blocking collectives: 107 us -> 107 us  [local(): sums = lax.psum(sums, mesh_axis)]
where the time goes in v1:
time: 392 us; the launch traced here: 390 us
  blocking collectives  222 us (57%)
  waiting for transfers between devices  49.2 us (13%)
  matrix products  38.7 us (10%)
  local copies, waits for them, and re-layouts  24.4 us (6%)
  starting transfers between devices  24.2 us (6%)
  other arithmetic  16.1 us (4%)
  between operations  15.3 us (4%)
    psum x2, blocking collectives, local(): sums = lax.psum(sums, mesh_axis)  107 us
    all_gather x3, blocking collectives, joined_2(): pieces = jax.tree.map(lambda part: lax.all_gather(part, axis), value)  54 us
    dot_general x2, matrix products, vocab_stats(): jnp.einsum('td,vd->tv', row_block, weights, preferred_element_type=jnp.fl...  26.9 us
    all_to_all x1, waiting for transfers between devices, local(): lax.all_to_all(outputs[:, :, slots:], 'ep', split_axis=0, concat_axis=0,...  21.1 us
    all_gather x1, blocking collectives, local(): lax.all_gather(ref_normed, 'grp', axis=0, tiled=True)  20.5 us
    unnamed x1, blocking collectives  20.4 us
    all_gather x1, blocking collectives, local(): lax.all_gather(pol_normed, 'grp', axis=0, tiled=True)  20.2 us
    all_to_all x1, waiting for transfers between devices, local(): lax.all_to_all(ref_send, 'ep', split_axis=0, concat_axis=0, tiled=True)  14.5 us
  transfers between devices with their start and end apart: 5, of which 3 were waited for; matrix products, arithmetic and copies ran while one was open for 9% of the time, Pallas kernels for 0%

profile of v1, /device:TPU:1, one launch (start us, length us, event | category | flops | bytes accessed | tf_op | source)
XLA Modules:
  0.0 390.0 jit_solution(1898214476692453274)
XLA Ops:
  11.8 2.0 copy.67
  13.7 8.7 %all-to-all-start = ((bf16[32,2,7,1024]{3,1,2,0:T(2,128)(2,1)}), bf16[32,2,7,1024]{3,1,2,0:T(2,128)(2,1)S(1)}, u32[]{:S(2)}, u32[]{:S(2)}) async-start(bf16[32,2,7,1024]{3,1,2,0:T(2,128)(2,1)} %copy.67), calls=%async_computation | async-start | bytes 1835008 | tf_op jit(solution)/shard_map/all_to_all | solution.py:81
  27.0 2.0 copy.71
  28.9 12.9 %all-to-all-done = bf16[32,2,7,1024]{3,1,2,0:T(2,128)(2,1)S(1)} async-done(((bf16[32,2,7,1024]{3,1,2,0:T(2,128)(2,1)}), bf16[32,2,7,1024]{3,1,2,0:T(2,128)(2,1)S(1)}, u32[]{:S(2)}, u32[]{:S(2)}) %all-to-all-start) | async-done | bytes 917536 | tf_op jit(solution)/shard_map/all_to_all | solution.py:81
  42.7 5.4 %all-to-all-start.1 = ((bf16[32,2,7,1024]{3,1,2,0:T(2,128)(2,1)}), bf16[32,2,7,1024]{3,1,2,0:T(2,128)(2,1)}, u32[]{:S(2)}, u32[]{:S(2)}) async-start(bf16[32,2,7,1024]{3,1,2,0:T(2,128)(2,1)} %copy.71), calls=%async_computation.1 | async-start | bytes 1835008 | tf_op jit(solution)/shard_map/all_to_all | solution.py:82
  49.6 14.5 %all-to-all-done.1 = bf16[32,2,7,1024]{3,1,2,0:T(2,128)(2,1)} async-done(((bf16[32,2,7,1024]{3,1,2,0:T(2,128)(2,1)}), bf16[32,2,7,1024]{3,1,2,0:T(2,128)(2,1)}, u32[]{:S(2)}, u32[]{:S(2)}) %all-to-all-start.1) | async-done | bytes 917536 | tf_op jit(solution)/shard_map/all_to_all | solution.py:82
  65.8 2.2 fusion.9
  68.0 5.2 %convert_bitcast_fusion = bf16[32,2,14,1024]{3,0,2,1:T(8,128)(2,1)} fusion(bf16[2,384,1024]{2,1,0:T(8,128)(2,1)S(1)} %copy-done, bf16[32,2,14,1024]{3,0,2,1:T(8,128)(2,1)S(1)} %copy_dynamic-update-slice_fusion, bf16[2,1024,384]{2,1,0:T(8,128)(2,1)} %param.23, f32[32,2,14,384]{3,0,2,1:T(8,128)} %fusion.9), kind=kOutput, calls=%fused_computation.12 | convolution fusion | flops 1412268032 | bytes 8192000 | tf_op jit(solution)/shard_map/nesf,efd->nesd/dot_general | solution.py:88
  73.2 1.9 fusion.44
  75.2 1.9 copy.78
  77.1 3.9 all-to-all-start.3
  83.7 21.1 %all-to-all-done.3 = bf16[32,2,7,1024]{3,1,2,0:T(2,128)(2,1)S(1)} async-done(((bf16[32,2,7,1024]{3,1,2,0:T(2,128)(2,1)}), bf16[32,2,7,1024]{3,1,2,0:T(2,128)(2,1)S(1)}, u32[]{:S(2)}, u32[]{:S(2)}) %all-to-all-start.3) | async-done | bytes 917536 | tf_op jit(solution)/shard_map/all_to_all | solution.py:92
  104.8 6.1 %all-to-all-start.2 = ((bf16[32,2,7,1024]{3,1,2,0:T(2,128)(2,1)}), bf16[32,2,7,1024]{3,1,2,0:T(2,128)(2,1)S(1)}, u32[]{:S(2)}, u32[]{:S(2)}) async-start(bf16[32,2,7,1024]{3,1,2,0:T(2,128)(2,1)} %copy.74), calls=%async_computation.2 | async-start | bytes 1835008 | tf_op jit(solution)/shard_map/all_to_all | solution.py:91
  113.7 20.4 %all-reduce = s32[320]{0:T(512)S(1)} all-reduce(s32[320]{0:T(512)S(1)} %dynamic-update-slice), channel_id=1, replica_groups=mesh['grp'=8,'ep'=32] {'grp'}, use_global_device_ids=true, to_apply=%add | all-reduce | flops 320 | bytes 2560
  141.2 20.2 %all_gather.26 = bf16[320,1024]{1,0:T(8,128)(2,1)S(1)} all-gather(bf16[40,1024]{1,0:T(8,128)(2,1)S(1)} %get-tuple-element.71), channel_id=1, replica_groups=mesh['grp'=8,'ep'=32] {'grp'}, dimensions={0}, use_global_device_ids=true | all-gather | bytes 737280 | tf_op jit(solution)/shard_map/all_gather | solution.py:107
  161.4 20.5 %all_gather.28 = bf16[320,1024]{1,0:T(8,128)(2,1)S(1)} all-gather(bf16[40,1024]{1,0:T(8,128)(2,1)S(1)} %get-tuple-element.72), channel_id=1, replica_groups=mesh['grp'=8,'ep'=32] {'grp'}, dimensions={0}, use_global_device_ids=true | all-gather | bytes 737280 | tf_op jit(solution)/shard_map/all_gather | solution.py:108
  181.9 13.4 %fusion.45 = (f32[320]{0:T(512)S(1)}, f32[320,9728]{1,0:T(8,128)}) fusion(bf16[320,1024]{1,0:T(8,128)(2,1)S(1)} %all_gather.26, bf16[9728,1024]{1,0:T(8,128)(2,1)} %all-gather.4.cloned.1.call-done), kind=kOutput, calls=%fused_computation.84 | convolution fusion | flops 6378454528 | bytes 33031424 | tf_op jit(solution)/shard_map/td,vd->tv/dot_general | solution.py:24
  195.3 13.5 %fusion.46 = (f32[320]{0:T(512)S(1)}, f32[320,9728]{1,0:T(8,128)}) fusion(bf16[320,1024]{1,0:T(8,128)(2,1)S(1)} %all_gather.28, bf16[9728,1024]{1,0:T(8,128)(2,1)} %all-gather.4.cloned.1.call-done), kind=kOutput, calls=%fused_computation.85 | convolution fusion | flops 6378454528 | bytes 33031424 | tf_op jit(solution)/shard_map/td,vd->tv/dot_general | solution.py:24
  208.8 11.5 %fusion.2 = (f32[320]{0:T(512)S(1)}, f32[320]{0:T(512)S(1)}, f32[320]{0:T(512)S(1)}, f32[320]{0:T(512)S(1)}) fusion(f32[320,9728]{1,0:T(8,128)} %get-tuple-element.80, s32[9728]{0:T(1024)S(1)} %copy-done.17, s32[320]{0:T(512)S(1)} %all-reduce, f32[320]{0:T(512)S(1)} %get-tuple-element.79, f32[320,9728]{1,0:T(8,128)} %get-tuple-element.82, ...), kind=kLoop, calls=%fused_computation.8 | loop fusion | flops 28015360 | bytes 24951552 | tf_op jit(solution)/shard_map/reduce_sum | solution.py:27
  220.3 18.0 %all-gather.1 = f32[8,2,320]{2,1,0:T(2,128)S(1)} all-gather(f32[1,2,320]{2,1,0:T(2,128)S(1)} %maximum_bitcast_fusion), channel_id=2, replica_groups=mesh['grp'=8,'ep'=32] {'grp'}, dimensions={0}, use_global_device_ids=true | all-gather | bytes 23040 | tf_op jit(solution)/shard_map/all_gather | solution.py:8
  238.4 18.0 %all_gather.30 = f32[8,2,320]{2,1,0:T(2,128)S(1)} all-gather(f32[1,2,320]{2,1,0:T(2,128)S(1)} %get-tuple-element.73), channel_id=1, replica_groups=mesh['grp'=8,'ep'=32] {'grp'}, dimensions={0}, use_global_device_ids=true | all-gather | bytes 23040 | tf_op jit(solution)/shard_map/all_gather | solution.py:8
  256.5 18.0 %all_gather.29 = f32[8,2,320]{2,1,0:T(2,128)S(1)} all-gather(f32[1,2,320]{2,1,0:T(2,128)S(1)} %get-tuple-element.74), channel_id=1, replica_groups=mesh['grp'=8,'ep'=32] {'grp'}, dimensions={0}, use_global_device_ids=true | all-gather | bytes 23040 | tf_op jit(solution)/shard_map/all_gather | solution.py:8
  275.7 94.9 %psum.14 = f32[256]{0:T(256)S(1)} all-reduce(f32[256]{0:T(256)S(1)} %convert_divide_fusion), channel_id=1, replica_groups=mesh['grp'=8,'ep'=32] {'ep'}, use_global_device_ids=true, to_apply=%region_18.19 | all-reduce | flops 256 | bytes 2048 | tf_op jit(solution)/shard_map/psum | solution.py:138
  370.5 12.0 %psum.15 = f32[256]{0:T(256)S(1)} all-reduce(f32[256]{0:T(256)S(1)} %psum.14), channel_id=1, replica_groups=mesh['grp'=8,'ep'=32] {'grp'}, use_global_device_ids=true, to_apply=%region_19.20 | all-reduce | flops 256 | bytes 2048 | tf_op jit(solution)/shard_map/psum | solution.py:138
  (150 shorter events, 26.8 us)
Async XLA Ops:
  7.2 60.8 %copy-start = (bf16[2,384,1024]{2,1,0:T(8,128)(2,1)S(1)}, bf16[2,384,1024]{2,1,0:T(8,128)(2,1)}, u32[]{:S(2)}) copy-start(bf16[2,384,1024]{2,1,0:T(8,128)(2,1)} %param.24) | copy-start | bytes 4718596
  7.2 3.8 copy-start.7
  7.2 174.7 %all-gather.4.cloned.1.call-start = ((), (), s32[]{:S(2)}) async-start(), calls=%async_computation.4 | async-start | bytes 20545536 | tf_op jit(solution)/shard_map/all_gather | solution.py:114
  11.7 10.7 %copy-start.22 = (s32[40,8]{0,1:T(8,128)S(1)}, s32[40,8]{0,1:T(8,128)}, u32[]{:S(2)}) copy-start(s32[40,8]{0,1:T(8,128)} %param.19) | copy-start | bytes 3844
  13.7 10.4 %copy-start.5 = (bf16[40,1024]{1,0:T(8,128)(2,1)S(1)}, bf16[40,1024]{1,0:T(8,128)(2,1)}, u32[]{:S(2)}) copy-start(bf16[40,1024]{1,0:T(8,128)(2,1)} %param.17) | copy-start | bytes 245764
  13.7 10.4 %copy-start.19 = (s32[448]{0:T(512)S(1)}, s32[448]{0:T(512)}, u32[]{:S(2)}) copy-start(s32[448]{0:T(512)} %copy-done.18) | copy-start | bytes 5380
  13.7 28.1 %all-to-all-start = ((bf16[32,2,7,1024]{3,1,2,0:T(2,128)(2,1)}), bf16[32,2,7,1024]{3,1,2,0:T(2,128)(2,1)S(1)}, u32[]{:S(2)}, u32[]{:S(2)}) async-start(bf16[32,2,7,1024]{3,1,2,0:T(2,128)(2,1)} %copy.67), calls=%async_computation | async-start | bytes 1835008 | tf_op jit(solution)/shard_map/all_to_all | solution.py:81
  42.7 21.4 %all-to-all-start.1 = ((bf16[32,2,7,1024]{3,1,2,0:T(2,128)(2,1)}), bf16[32,2,7,1024]{3,1,2,0:T(2,128)(2,1)}, u32[]{:S(2)}, u32[]{:S(2)}) async-start(bf16[32,2,7,1024]{3,1,2,0:T(2,128)(2,1)} %copy.71), calls=%async_computation.1 | async-start | bytes 1835008 | tf_op jit(solution)/shard_map/all_to_all | solution.py:82
  75.2 5.8 %copy-start.23 = (f32[40,8]{0,1:T(8,128)S(1)}, f32[40,8]{0,1:T(8,128)}, u32[]{:S(2)}) copy-start(f32[40,8]{0,1:T(8,128)} %param.21) | copy-start | bytes 3844
  75.2 5.9 %copy-start.16 = (s32[40,8]{1,0:T(8,128)S(1)}, s32[40,8]{1,0:T(8,128)}, u32[]{:S(2)}) copy-start(s32[40,8]{1,0:T(8,128)} %copy-done.15) | copy-start | bytes 3844
  75.2 6.1 %copy-start.12 = (s32[40,64]{0,1:T(8,128)S(1)}, s32[40,64]{0,1:T(8,128)}, u32[]{:S(2)}) copy-start(s32[40,64]{0,1:T(8,128)} %copy-done.11) | copy-start | bytes 30724
  77.1 4.4 %copy-start.24 = (f32[40,8]{0,1:T(8,128)S(1)}, f32[40,8]{0,1:T(8,128)}, u32[]{:S(2)}) copy-start(f32[40,8]{0,1:T(8,128)} %param.20) | copy-start | bytes 3844
  77.1 4.4 %copy-start.14 = (s32[40,8]{1,0:T(8,128)S(1)}, s32[40,8]{1,0:T(8,128)}, u32[]{:S(2)}) copy-start(s32[40,8]{1,0:T(8,128)} %copy-done.13) | copy-start | bytes 3844
  77.1 27.7 %all-to-all-start.3 = ((bf16[32,2,7,1024]{3,1,2,0:T(2,128)(2,1)}), bf16[32,2,7,1024]{3,1,2,0:T(2,128)(2,1)S(1)}, u32[]{:S(2)}, u32[]{:S(2)}) async-start(bf16[32,2,7,1024]{3,1,2,0:T(2,128)(2,1)} %copy.78), calls=%async_computation.3 | async-start | bytes 1835008 | tf_op jit(solution)/shard_map/all_to_all | solution.py:92
  81.8 29.2 %copy-start.10 = (s32[40,64]{0,1:T(8,128)S(1)}, s32[40,64]{0,1:T(8,128)}, u32[]{:S(2)}) copy-start(s32[40,64]{0,1:T(8,128)} %copy-done.9) | copy-start | bytes 30724
  81.8 30.0 %copy-start.20 = (s32[256]{0:T(256)S(1)}, s32[256]{0:T(256)}, u32[]{:S(2)}) copy-start(s32[256]{0:T(256)} %param.28) | copy-start | bytes 3076
  81.8 30.4 %copy-start.28 = (u32[256]{0:T(256)S(1)}, u32[256]{0:T(256)}, u32[]{:S(2)}) copy-start(u32[256]{0:T(256)} %constant.68) | copy-start | bytes 3076
  81.8 31.6 %copy-start.27 = (s32[40]{0:T(128)S(1)}, s32[40]{0:T(128)}, u32[]{:S(2)}) copy-start(s32[40]{0:T(128)} %param.27) | copy-start | bytes 484
  104.8 32.7 %all-to-all-start.2 = ((bf16[32,2,7,1024]{3,1,2,0:T(2,128)(2,1)}), bf16[32,2,7,1024]{3,1,2,0:T(2,128)(2,1)S(1)}, u32[]{:S(2)}, u32[]{:S(2)}) async-start(bf16[32,2,7,1024]{3,1,2,0:T(2,128)(2,1)} %copy.74), calls=%async_computation.2 | async-start | bytes 1835008 | tf_op jit(solution)/shard_map/all_to_all | solution.py:91
  195.3 13.5 %copy-start.17 = (s32[9728]{0:T(1024)S(1)}, s32[9728]{0:T(1024)}, u32[]{:S(2)}) copy-start(s32[9728]{0:T(1024)} %iota_add_fusion) | copy-start | bytes 116740
  208.8 66.7 %copy-start.26 = (s32[256]{0:T(256)S(1)}, s32[256]{0:T(256)}, u32[]{:S(2)}) copy-start(s32[256]{0:T(256)} %get-tuple-element.67) | copy-start | bytes 3076
  208.8 66.7 %copy-start.29 = (s32[40]{0:T(128)S(1)}, s32[40]{0:T(128)}, u32[]{:S(2)}) copy-start(s32[40]{0:T(128)} %iota_add_fusion.1) | copy-start | bytes 484
  208.8 173.7 %copy-start.25 = (s32[256]{0:T(256)S(1)}, s32[256]{0:T(256)}, u32[]{:S(2)}) copy-start(s32[256]{0:T(256)} %param.29) | copy-start | bytes 3076
  208.8 174.3 %copy-start.1 = (bf16[2,384,1024]{2,1,0:T(8,128)(2,1)S(1)}, bf16[2,384,1024]{2,1,0:T(8,128)(2,1)}, u32[]{:S(2)}) copy-start(bf16[2,384,1024]{2,1,0:T(8,128)(2,1)} %param.24) | copy-start | bytes 4718596
  (11 other events, 12.0 us)
Sparse Core Ops, SparseCore 0:
  10.6 105.0 all-gather.3
